TPU v7x, 32 devices: a whole 2x2x4 slice. The times are simulated.
32 devices in a mesh: layer: 8 (over z, y), latent: 4 (over x, core).
Axes of the slice: x: 2, y: 2, z: 4, core: 2. Of those that a mesh axis runs over, the one named last changes fastest.
Arguments:
- layer_inputs: bfloat16 [384, 8192], P('latent', 'layer'), may hold values from -6 to 6
- mlp_outputs: bfloat16 [384, 8192], P('latent', 'layer'), may hold values from -6 to 6
- enc_weight: bfloat16 [8192, 4096], P('layer', 'latent'), may hold values from -0.125 to 0.125
- enc_bias: float32 [4, 4096], P(None, 'latent'), may hold values from -1 to 0.5
- dec_weight: bfloat16 [4, 4096, 8192], P(None, 'latent', 'layer'), may hold values from -0.046875 to 0.046875
Outputs:
- enc_grad: float32 [8192, 4096], P('layer', 'latent')
- dec_grad: bfloat16 [4, 4096, 8192], P(None, 'latent', 'layer')
All inputs are finite; a program needn't handle non-finite values.
Results may differ from a plain program's by a relative error of at most 0.011.
Values may be sent and summed in bfloat16 or wider, within the bound.
A program may use at most 64 MiB of HBM per device.

v0:
```python
import functools

import jax
import jax.numpy as jnp
from jax import lax
from jax.experimental import pallas as pl
from jax.experimental.pallas import tpu as pltpu
from jax.sharding import PartitionSpec as P

MESH = pl.DeviceIdType.MESH
F32 = jnp.float32
BF16 = jnp.bfloat16


def exchange_kernel(
    layers, blocks, rscale,
    x_hbm, mlp_hbm, w_hbm, bias_hbm, v_hbm,
    dec_out, xg_out, pg_out,
    xg, mlp, w, bias_all, v, part_send, part_recv, pre, lat, recon, core_send, core_recv, rs_send, rs_recv, og,
    bys, byr, bown, bof, bzs, bzr, bzso, bzro, pg, dec,
    x_ss, x_rs, p_ss, p_rs, z_ss, z_rs, zo_ss, zo_rs, y_ss, y_rs, core_ss, core_rs, rs_ss, rs_rs, og_ss, og_fs, og_rs,
    by_ss, by_rs, bz_ss, bz_rs, bzo_ss, bzo_rs, f_ss, f_rs, in_sem, dec_sem, out_sem,
):
    p = lax.axis_index("layer")
    q = lax.axis_index("latent")
    t = p // 2
    y = p % 2
    o = 1 - y
    rb = x_hbm.shape[0]
    half = w.shape[1] // 2
    partner = (p + 1 - 2 * y, q)
    up = (p + 2, q)
    down = (p - 2, q)
    chips = blocks // 2

    def blk(k):
        return ((q // 2 + k // 2) % chips) * 2 + (q % 2 + k % 2) % 2

    def rows(b):
        return pl.ds(pl.multiple_of(b * rb, rb), rb)

    def cols(h):
        return pl.ds(pl.multiple_of(h * half, half), half)

    def rcopy(src, dst, ss, rs, dev):
        return pltpu.make_async_remote_copy(
            src_ref=src, dst_ref=dst, send_sem=ss, recv_sem=rs, device_id=dev, device_id_type=MESH
        )

    own_x = pltpu.make_async_copy(x_hbm, xg.at[rows(q)], in_sem.at[0])
    w_copy = pltpu.make_async_copy(w_hbm, w, in_sem.at[1])
    bias_copy = pltpu.make_async_copy(bias_hbm, bias_all, in_sem.at[2])
    mlp_copy = pltpu.make_async_copy(mlp_hbm, mlp, in_sem.at[3])
    v_copy = pltpu.make_async_copy(v_hbm, v, in_sem.at[4])
    for copy in (own_x, w_copy, bias_copy, mlp_copy, v_copy):
        copy.start()
    both_up = list(range(blocks - max(blocks // 4, 1), blocks))
    one_up = list(range(blocks - max(blocks // 4, 1)))
    both_down = list(range(blocks - max(blocks // 4, 1), blocks))
    one_down = list(range(blocks - max(blocks // 4, 1)))

    barrier = pltpu.get_barrier_semaphore()
    for k in range(1, blocks):
        pl.semaphore_signal(barrier, inc=1, device_id=(p, blk(k)), device_id_type=MESH)
    pl.semaphore_signal(barrier, inc=1, device_id=partner, device_id_type=MESH)

    @pl.when(t < layers - 1)
    def _():
        pl.semaphore_signal(barrier, inc=1, device_id=up, device_id_type=MESH)

    @pl.when(t > 0)
    def _():
        pl.semaphore_signal(barrier, inc=1, device_id=down, device_id_type=MESH)

    neighbours = blocks + (t < layers - 1).astype(jnp.int32) + (t > 0).astype(jnp.int32)
    pl.semaphore_wait(barrier, neighbours)

    def x_copy(k):
        return rcopy(x_hbm, xg.at[rows(q)], x_ss.at[k], x_rs.at[q], (p, blk(k)))

    for k in list(range(2, blocks)) + [1]:
        x_copy(k).start()

    def part_copy(b):
        return rcopy(part_send.at[rows(b)], part_recv.at[rows(b)], p_ss.at[b], p_rs.at[b], partner)

    def lat_up(l, b):
        piece = lat.at[l, y, rows(b)]
        return rcopy(piece, piece, z_ss.at[l, b], z_rs.at[l, b], up)

    def lat_up_other(l, b):
        piece = lat.at[l, o, rows(b)]
        return rcopy(piece, piece, zo_ss.at[l, b], zo_rs.at[l, b], up)

    def lat_swap(l, b):
        piece = lat.at[l, y, rows(b)]
        return rcopy(piece, piece, y_ss.at[l, b], y_rs.at[l, b], partner)

    def lat_swap_in(l, b):
        piece = lat.at[l, o, rows(b)]
        return rcopy(piece, piece, y_ss.at[l, b], y_rs.at[l, b], partner)

    def own_block(b):
        part_copy(b).wait_recv()
        total = pre[rows(b), :] + part_recv[rows(b), :] + bias
        pre[rows(b), :] = total
        lat[t, y, rows(b), :] = jnp.maximum(total, 0.0).astype(BF16)

        @pl.when(t < layers - 1)
        def _():
            lat_up(t, b).start()

        lat_swap(t, b).start()

    def relay(l, k):
        b = blk(k)
        lat_up(l, b).wait_recv()

        @pl.when(t < layers - 1)
        def _():
            lat_up(l, b).start()

        if k in one_up:
            lat_swap(l, b).start()

    def relay_below(k):
        @pl.when(t > 0)
        def _():
            relay(t - 1, k)

    bias_copy.wait()
    bias_half = jnp.where(y == 0, bias_all[:, :half], bias_all[:, half:])
    own_row = lax.broadcasted_iota(jnp.int32, bias_half.shape, 0) == t
    bias = jnp.sum(jnp.where(own_row, bias_half, 0.0), axis=0, keepdims=True)
    own_x.wait()
    w_copy.wait()
    for k in range(blocks):
        b = blk(k)
        if k > 0:
            rcopy(x_hbm, xg.at[rows(b)], x_ss.at[k], x_rs.at[b], (p, b)).wait_recv()
        part_send[rows(b), :] = jnp.dot(xg[rows(b), :], w[:, cols(o)], preferred_element_type=F32)
        part_copy(b).start()
        pre[rows(b), :] = jnp.dot(xg[rows(b), :], w[:, cols(y)], preferred_element_type=F32)
        if k > 0:
            own_block(blk(k - 1))
        if k > 1:
            relay_below(k - 2)
    own_block(blk(blocks - 1))
    relay_below(blocks - 2)
    relay_below(blocks - 1)
    xg_copy = pltpu.make_async_copy(xg, xg_out, out_sem.at[0])
    xg_copy.start()

    recon[...] = jnp.zeros_like(recon)
    v_copy.wait()

    def decode(l, h):
        recon[...] += jnp.dot(lat[l, h], v[l, cols(h), :], preferred_element_type=F32)

    def other_up(l, b):
        @pl.when(t < layers - 1)
        def _():
            lat_up_other(l, b).start()

    def forward(s, carry):
        l = t - s

        @pl.when(jnp.logical_and(s > 1, s <= t))
        def _():
            for k in range(blocks):
                relay(l, k)

        @pl.when(s <= t)
        def _():
            decode(l, y)

        @pl.when(s > 0)
        def _():
            for k in both_up:
                b = blk(k)

                @pl.when(s == 1)
                def _():
                    lat_swap_in(t, b).wait_recv()

                @pl.when(s > 1)
                def _():
                    lat_up_other(l + 1, b).wait_recv()

                other_up(l + 1, b)
            for k in one_up:
                lat_swap_in(l + 1, blk(k)).wait_recv()
            decode(l + 1, o)

        return carry

    lax.fori_loop(0, t + 2, forward, 0)

    def core_copy(c):
        return rcopy(core_send.at[c], core_recv.at[c], core_ss.at[c], core_rs.at[c], (p, blk(1)))

    def rs_copy(c):
        return rcopy(rs_send.at[c], rs_recv.at[q // 2], rs_ss.at[c], rs_rs.at[q // 2], (p, blk(2 * c)))

    def rs_in(c):
        chip = (q // 2 + c) % chips
        return rcopy(rs_send.at[c], rs_recv.at[chip], rs_ss.at[c], rs_rs.at[chip], (p, blk(2 * c)))

    order = list(range(1, chips)) + [0]
    for c in order:
        core_send[c] = recon[rows(blk(2 * c + 1)), :].astype(BF16)
        core_copy(c).start()
    for c in order:
        core_copy(c).wait_recv()
        total = recon[rows(blk(2 * c)), :] + core_recv[c].astype(F32)
        if c > 0:
            rs_send[c] = total.astype(BF16)
            rs_copy(c).start()
    mlp_copy.wait()
    for c in range(1, chips):
        rs_in(c).wait_recv()
        total = total + rs_recv[(q // 2 + c) % chips].astype(F32)
    og[rows(q), :] = ((total - mlp[...].astype(F32)) * rscale).astype(BF16)

    def og_copy(src, ss, k):
        return rcopy(og.at[rows(src)], og.at[rows(src)], ss.at[k], og_rs.at[src], (p, blk(k)))

    def og_relay(k):
        return rcopy(og.at[rows(blk(k))], og.at[rows(blk(k))], og_fs.at[k], og_rs.at[blk(k)], (p, blk(1)))

    for k in list(range(2, blocks, 2)) + [1]:
        og_copy(q, og_ss, k).start()
    for k in range(2, blocks, 2):
        og_copy(blk(k), og_ss, k).wait_recv()
        og_relay(k).start()
    for k in range(1, blocks, 2):
        og_copy(blk(k), og_ss, k).wait_recv()

    def by_copy(l, b):
        return rcopy(bys.at[l, rows(b)], byr.at[l, rows(b)], by_ss.at[l, b], by_rs.at[l, b], partner)

    def bz_copy(l, b):
        return rcopy(bzs.at[l, rows(b)], bzr.at[l, rows(b)], bz_ss.at[l, b], bz_rs.at[l, b], down)

    def bz_other(l, b):
        return rcopy(bzso.at[l, rows(b)], bzro.at[l, rows(b)], bzo_ss.at[l, b], bzo_rs.at[l, b], down)

    def dec_copy(l):
        return pltpu.make_async_copy(dec.at[l], dec_out.at[l], dec_sem.at[l])

    def back(l, h):
        return lax.dot_general(
            og[...], v[l, cols(h), :], (((1,), (1,)), ((), ())), preferred_element_type=F32
        )

    def add_own(l, b):
        bz_copy(l, b).wait_recv()
        bown[l, rows(b), :] += bzr[l, rows(b), :].astype(F32)

    def add_other(l, b):
        bz_other(l, b).wait_recv()
        bof[l, rows(b), :] += bzro[l, rows(b), :].astype(F32)

    def send_both(l, b):
        bzs[l, rows(b), :] = bown[l, rows(b), :].astype(BF16)
        bz_copy(l, b).start()
        bzso[l, rows(b), :] = bof[l, rows(b), :].astype(BF16)
        bz_other(l, b).start()

    def swap_sum(l, b):
        bys[l, rows(b), :] = bof[l, rows(b), :].astype(BF16)
        by_copy(l, b).start()

    def produce(l, carry):
        bof[l] = back(l, o)

        @pl.when(jnp.logical_and(t == layers - 1, l == t))
        def _():
            for k in both_down:
                swap_sum(l, blk(k))

        for k in one_down:
            swap_sum(l, blk(k))
        bown[l] = back(l, y)

        @pl.when(t == layers - 1)
        def _():
            for k in both_down:
                b = blk(k)

                @pl.when(l < t)
                def _():
                    send_both(l, b)

        return carry

    lax.fori_loop(0, t + 1, produce, 0)

    def collected(l, b):
        by_copy(l, b).wait_recv()
        return bown[l, rows(b), :] + byr[l, rows(b), :].astype(F32)

    def dec_piece(l):
        for h in range(2):
            piece = lax.dot_general(
                lat[l, h], og[...], (((0,), (0,)), ((), ())), preferred_element_type=F32
            )
            dec[l, h * half:(h + 1) * half, :] = piece.astype(BF16)
        dec_copy(l).start()

    def combine_both(l, carry):
        for k in both_down:
            b = blk(k)
            add_own(l, b)
            add_other(l, b)

            @pl.when(l < t)
            def _():
                send_both(l, b)

            @pl.when(l == t)
            def _():
                swap_sum(l, b)

        return carry

    @pl.when(t < layers - 1)
    def _():
        lax.fori_loop(0, t + 1, combine_both, 0)

    def combine(l, carry):
        @pl.when(l < t)
        def _():
            for k in one_down:
                b = blk(k)

                @pl.when(t < layers - 1)
                def _():
                    add_own(l, b)

                bzs[l, rows(b), :] = collected(l, b).astype(BF16)
                bz_copy(l, b).start()

        dec_piece(l)
        return carry

    lax.fori_loop(0, t + 1, combine, 0)

    def blank(l, carry):
        dec[l] = jnp.zeros((2 * half, dec.shape[2]), BF16)
        dec_copy(l).start()
        return carry

    lax.fori_loop(t + 1, layers, blank, 0)

    def final_copy(h, b):
        piece = pg.at[h, rows(b)]
        return rcopy(piece, piece, f_ss.at[b], f_rs.at[b], partner)

    for k in both_down + one_down:
        b = blk(k)
        if k in one_down:
            @pl.when(t < layers - 1)
            def _():
                add_own(t, b)

        value = jnp.where(pre[rows(b), :] > 0.0, collected(t, b), 0.0)
        pg[y, rows(b), :] = value.astype(BF16)
        final_copy(y, b).start()
    for b in range(blocks):
        final_copy(o, b).wait_recv()
    own_dma = pltpu.make_async_copy(pg.at[y], pg_out.at[:, cols(y)], out_sem.at[1])
    other_dma = pltpu.make_async_copy(pg.at[o], pg_out.at[:, cols(o)], out_sem.at[2])
    own_dma.start()
    other_dma.start()

    for k in range(1, blocks):
        x_copy(k).wait_send()
    for c in range(chips):
        core_copy(c).wait_send()
        if c > 0:
            rs_copy(c).wait_send()
    for k in list(range(2, blocks, 2)) + [1]:
        og_copy(q, og_ss, k).wait_send()
    for k in range(2, blocks, 2):
        og_relay(k).wait_send()
    for b in range(blocks):
        part_copy(b).wait_send()
        final_copy(y, b).wait_send()

    def drain(l, carry):
        for k in range(blocks):
            b = blk(k)

            @pl.when(jnp.logical_or(l == t, k in one_up))
            def _():
                lat_swap(l, b).wait_send()

            @pl.when(jnp.logical_or(l == t, k in one_down))
            def _():
                by_copy(l, b).wait_send()

            @pl.when(t < layers - 1)
            def _():
                lat_up(l, b).wait_send()
                if k in both_up:
                    lat_up_other(l, b).wait_send()

            @pl.when(l < t)
            def _():
                bz_copy(l, b).wait_send()
                if k in both_down:
                    bz_other(l, b).wait_send()

        return carry

    lax.fori_loop(0, t + 1, drain, 0)
    for l in range(layers):
        dec_copy(l).wait()
    xg_copy.wait()
    own_dma.wait()
    other_dma.wait()


def exchange(layer_inputs, mlp_outputs, enc_weight, enc_bias, dec_weight):
    layers, latents, width = dec_weight.shape
    blocks = lax.axis_size("latent")
    rb, depth = layer_inputs.shape
    total_rows = rb * blocks
    half = latents // 2
    rscale = total_rows ** (-0.5)
    hbm = pl.BlockSpec(memory_space=pltpu.HBM)
    dma = pltpu.SemaphoreType.DMA
    per_block = dma((blocks,))
    per_layer = dma((layers, blocks))
    sums = pltpu.VMEM((layers, total_rows, half), F32)
    sent = pltpu.VMEM((layers, total_rows, half), BF16)
    one_half = pltpu.VMEM((total_rows, half), F32)
    row_blocks = pltpu.VMEM((blocks // 2, rb, width), BF16)
    per_chip = dma((blocks // 2,))
    return pl.pallas_call(
        functools.partial(exchange_kernel, layers, blocks, rscale),
        out_shape=(
            jax.ShapeDtypeStruct((layers, latents, width), BF16),
            jax.ShapeDtypeStruct((total_rows, depth), BF16),
            jax.ShapeDtypeStruct((total_rows, latents), BF16),
        ),
        in_specs=[hbm] * 5,
        out_specs=(pl.BlockSpec(memory_space=pl.ANY),) * 3,
        scratch_shapes=[
            pltpu.VMEM((total_rows, depth), BF16),
            pltpu.VMEM((rb, width), BF16),
            pltpu.VMEM((depth, latents), BF16),
            pltpu.VMEM((layers, latents), F32),
            pltpu.VMEM((layers, latents, width), BF16),
            one_half, one_half, one_half,
            pltpu.VMEM((layers, 2, total_rows, half), BF16),
            pltpu.VMEM((total_rows, width), F32),
            row_blocks, row_blocks, row_blocks, row_blocks,
            pltpu.VMEM((total_rows, width), BF16),
            sent, sent, sums, sums, sent, sent, sent, sent,
            pltpu.VMEM((2, total_rows, half), BF16),
            pltpu.VMEM((layers, latents, width), BF16),
            per_block, per_block, per_block, per_block,
            per_layer, per_layer, per_layer, per_layer, per_layer, per_layer,
            per_chip, per_chip, per_chip, per_chip, per_block, per_block, per_block,
            per_layer, per_layer, per_layer, per_layer, per_layer, per_layer,
            per_block, per_block,
            dma((5,)), dma((layers,)), dma((3,)),
        ],
        compiler_params=pltpu.CompilerParams(
            collective_id=0, has_side_effects=True, vmem_limit_bytes=56 * 2**20
        ),
        name="exchange",
    )(layer_inputs, mlp_outputs, enc_weight, enc_bias, dec_weight)


def finish_kernel(
    xg_hbm, pg_hbm, dec_hbm, enc_out, dec_out, xg, pg, enc, dec, in_sem, dec_in, dec_sem, enc_sem
):
    layers = dec.shape[0]
    piece = enc.shape[0] // layers
    ins = [
        pltpu.make_async_copy(xg_hbm, xg, in_sem.at[0]),
        pltpu.make_async_copy(pg_hbm, pg, in_sem.at[1]),
    ]
    reads = [pltpu.make_async_copy(dec_hbm.at[l], dec.at[l], dec_in.at[l]) for l in range(layers)]
    for copy in ins + reads:
        copy.start()
    for copy in ins:
        copy.wait()
    writes = []
    for l in range(layers):
        part = pl.ds(l * piece, piece)
        enc[part, :] = lax.dot_general(
            xg[:, part], pg[...], (((0,), (0,)), ((), ())), preferred_element_type=F32
        )
        writes.append(pltpu.make_async_copy(enc.at[part], enc_out.at[part], enc_sem.at[l]))
        writes[-1].start()
        reads[l].wait()
        writes.append(pltpu.make_async_copy(dec.at[l], dec_out.at[l], dec_sem.at[l]))
        writes[-1].start()
    for copy in writes:
        copy.wait()


def local(layer_inputs, mlp_outputs, enc_weight, enc_bias, dec_weight):
    dec, xg, pg = exchange(layer_inputs, mlp_outputs, enc_weight, enc_bias, dec_weight)
    hbm = pl.BlockSpec(memory_space=pltpu.HBM)
    per_layer = pltpu.SemaphoreType.DMA((dec.shape[0],))
    return pl.pallas_call(
        finish_kernel,
        in_specs=[hbm] * 3,
        out_specs=(hbm,) * 2,
        out_shape=(
            jax.ShapeDtypeStruct(enc_weight.shape, F32),
            jax.ShapeDtypeStruct(dec_weight.shape, BF16),
        ),
        scratch_shapes=[
            pltpu.VMEM(xg.shape, BF16),
            pltpu.VMEM(pg.shape, BF16),
            pltpu.VMEM(enc_weight.shape, F32),
            pltpu.VMEM(dec.shape, BF16),
            pltpu.SemaphoreType.DMA((2,)),
            per_layer, per_layer, per_layer,
        ],
        compiler_params=pltpu.CompilerParams(vmem_limit_bytes=56 * 2**20),
        name="finish",
    )(xg, pg, dec)


def solution(mesh):
    in_specs = (
        P("latent", "layer"),
        P("latent", "layer"),
        P("layer", "latent"),
        P(None, "latent"),
        P(None, "latent", "layer"),
    )
    out_specs = (P("layer", "latent"), P(None, "latent", "layer"))
    return jax.shard_map(local, mesh=mesh, in_specs=in_specs, out_specs=out_specs, check_vma=False)
```

profile of v0, /device:TPU:20, one launch (start us, length us, event | category | flops | bytes accessed | tf_op | source)
XLA Modules:
  0.0 118.7 jit_solution(15190718925973886564)
XLA Ops:
  0.6 109.6 %exchange.1 = (bf16[4,1024,1024]{2,1,0:T(8,128)(2,1)}, bf16[384,1024]{1,0:T(8,128)(2,1)}, bf16[384,1024]{1,0:T(8,128)(2,1)}) custom-call(bf16[96,1024]{1,0:T(8,128)(2,1)} %x_hbm.1, bf16[96,1024]{1,0:T(8,128)(2,1)} %mlp_hbm.1, bf16[1024,1024]{1,0:T(8,128)(2,1)} %w_hbm.1, f32[4,1024]{1,0:T(4,128)} %bias_hbm.1, bf16[4,1024,1024]{2,1,0:T(8,128)(2,1)} %v_hbm.1), custom_call_target="tpu_custom_call" | custom-call | tf_op jit(solution)/shard_map/exchange/pallas_call | solution.py:441
  110.3 8.4 %finish.1 = (f32[1024,1024]{1,0:T(8,128)}, bf16[4,1024,1024]{2,1,0:T(8,128)(2,1)}) custom-call(bf16[384,1024]{1,0:T(8,128)(2,1)} %get-tuple-element.5.xg_hbm, bf16[384,1024]{1,0:T(8,128)(2,1)} %get-tuple-element.6.pg_hbm, bf16[4,1024,1024]{2,1,0:T(8,128)(2,1)} %get-tuple-element.7.dec_hbm), custom_call_target="tpu_custom_call" | custom-call | tf_op jit(solution)/shard_map/finish/pallas_call | solution.py:511
where the time goes:
time: 119 us
  Pallas kernels  118 us (99%)
    pallas_call x1, Pallas kernels, exchange(): pl.pallas_call(functools.partial(exchange_kernel, layers, blocks, rscale)...  110 us
    pallas_call x1, Pallas kernels, local(): pl.pallas_call(finish_kernel, in_specs=[hbm] * 3, out_specs=(hbm,) * 2, o...  8.41 us

commit v1 on v0

v1 whole, which is shorter than its diff:
```python
import functools

import jax
import jax.numpy as jnp
from jax import lax
from jax.experimental import pallas as pl
from jax.experimental.pallas import tpu as pltpu
from jax.sharding import PartitionSpec as P

MESH = pl.DeviceIdType.MESH
F32 = jnp.float32
BF16 = jnp.bfloat16
CHUNKS = (6, 3, 2)


def exchange_kernel(
    layers, blocks, chunks, rscale,
    x_hbm, mlp_hbm, w_hbm, bias_hbm, v_hbm,
    dec_out, xg_out, pg_out,
    xg, mlp, w, bias_all, v, pre, his, hir, los, lor, lat, recon, rss, rsr, og, acc, zds, zdr, ys, yr, pg, dec,
    x_ss, x_rs, hi_ss, hi_rs, lo_ss, lo_rs, zu_ss, zu_rs, rs_ss, rs_rs, og_ss, og_rs, zd_ss, zd_rs, y_ss, y_rs,
    own_sem, in_sem, dec_sem, out_sem,
):
    p = lax.axis_index("layer")
    q = lax.axis_index("latent")
    t = p // 2
    y = p % 2
    n = chunks
    top = layers - 1
    last = t == top
    below = t < top
    s = x_hbm.shape[0] // n
    size = s * blocks
    half = w.shape[1] // 2
    partner = (p + 1 - 2 * y, q)
    up = (p + 2, q)
    down = (p - 2, q)
    chips = blocks // 2

    def blk(k):
        return ((q // 2 + k // 2) % chips) * 2 + (q % 2 + k % 2) % 2

    def span(j):
        return pl.ds(pl.multiple_of(j * size, size), size)

    def piece(j, b):
        return pl.ds(pl.multiple_of(j * size + b * s, s), s)

    def mine(j):
        return pl.ds(pl.multiple_of(j * s, s), s)

    def rcopy(src, dst, ss, rs, dev):
        return pltpu.make_async_remote_copy(
            src_ref=src, dst_ref=dst, send_sem=ss, recv_sem=rs, device_id=dev, device_id_type=MESH
        )

    def loop(lower, upper, step):
        def body(i, carry):
            step(i)
            return carry

        lax.fori_loop(lower, upper, body, 0)

    def own_x(j):
        return pltpu.make_async_copy(x_hbm.at[mine(j)], xg.at[piece(j, q)], own_sem.at[j])

    w_copy = pltpu.make_async_copy(w_hbm, w, in_sem.at[0])
    bias_copy = pltpu.make_async_copy(bias_hbm, bias_all, in_sem.at[1])
    mlp_copy = pltpu.make_async_copy(mlp_hbm, mlp, in_sem.at[2])
    v_copy = pltpu.make_async_copy(v_hbm, v, in_sem.at[3])
    for j in range(n):
        own_x(j).start()
    for copy in (w_copy, bias_copy, mlp_copy, v_copy):
        copy.start()

    barrier = pltpu.get_barrier_semaphore()
    for k in range(1, blocks):
        pl.semaphore_signal(barrier, inc=1, device_id=(p, blk(k)), device_id_type=MESH)
    pl.semaphore_signal(barrier, inc=1, device_id=partner, device_id_type=MESH)

    @pl.when(below)
    def _():
        pl.semaphore_signal(barrier, inc=1, device_id=up, device_id_type=MESH)

    @pl.when(t > 0)
    def _():
        pl.semaphore_signal(barrier, inc=1, device_id=down, device_id_type=MESH)

    neighbours = blocks + below.astype(jnp.int32) + (t > 0).astype(jnp.int32)
    pl.semaphore_wait(barrier, neighbours)

    others = list(range(2, blocks)) + [1]

    def x_copy(j, k):
        return rcopy(x_hbm.at[mine(j)], xg.at[piece(j, q)], x_ss.at[j, k], x_rs.at[j, q], (p, blk(k)))

    def x_in(j, k):
        b = blk(k)
        return rcopy(x_hbm.at[mine(j)], xg.at[piece(j, b)], x_ss.at[j, k], x_rs.at[j, b], (p, b))

    def send_x(j):
        for k in others:
            x_copy(j, k).start()

    loop(0, n, send_x)

    def hi_copy(j):
        return rcopy(his.at[span(j)], hir.at[span(j)], hi_ss.at[j], hi_rs.at[j], partner)

    def lo_copy(j):
        return rcopy(los.at[span(j)], lor.at[span(j)], lo_ss.at[j], lo_rs.at[j], partner)

    def encode(j):
        own_x(j).wait()
        for k in others:
            x_in(j, k).wait_recv()
        part = jnp.dot(xg[span(j), :], w[...], preferred_element_type=F32)
        pre[span(j), :] = part
        hi = part.astype(BF16)
        his[span(j), :] = hi
        hi_copy(j).start()
        los[span(j), :] = (part - hi.astype(F32)).astype(BF16)

    def zu_copy(l, j):
        part = lat.at[l, :, span(j)]
        return rcopy(part, part, zu_ss.at[l, j], zu_rs.at[l, j], up)

    bias_copy.wait()
    own_row = lax.broadcasted_iota(jnp.int32, bias_all.shape, 0) == t
    bias = jnp.sum(jnp.where(own_row, bias_all[...], 0.0), axis=0, keepdims=True)
    w_copy.wait()
    ahead = min(n, 2)
    loop(0, ahead, encode)

    def decoded(l, j):
        return jnp.dot(lat[l, 0, span(j)], v[l, :half, :], preferred_element_type=F32) + jnp.dot(
            lat[l, 1, span(j)], v[l, half:, :], preferred_element_type=F32
        )

    def own_latents(j):
        hi_copy(j).wait_recv()
        total = pre[span(j), :] + hir[span(j), :].astype(F32) + bias
        pre[span(j), :] = total
        value = jnp.maximum(total, 0.0).astype(BF16)
        lat[t, 0, span(j)] = value[:, :half]
        lat[t, 1, span(j)] = value[:, half:]

        @pl.when(below)
        def _():
            zu_copy(t, j).start()

        recon[span(j), :] = decoded(t, j)
        lo_copy(j).start()

    def relay(l, j):
        zu_copy(l, j).wait_recv()

        @pl.when(below)
        def _():
            zu_copy(l, j).start()

        recon[span(j), :] += decoded(l, j)

    def rs_copy(j, k):
        b = blk(k)
        return rcopy(rss.at[piece(j, b)], rsr.at[q, mine(j)], rs_ss.at[j, k], rs_rs.at[j, q], (p, b))

    def rs_in(j, k):
        b = blk(k)
        return rcopy(rss.at[piece(j, b)], rsr.at[b, mine(j)], rs_ss.at[j, k], rs_rs.at[j, b], (p, b))

    def send_sums(j):
        rss[span(j), :] = recon[span(j), :].astype(BF16)
        for k in others:
            rs_copy(j, k).start()

    def og_copy(j, k):
        part = og.at[piece(j, q)]
        return rcopy(part, part, og_ss.at[j, k], og_rs.at[j, q], (p, blk(k)))

    def og_in(j, k):
        b = blk(k)
        part = og.at[piece(j, b)]
        return rcopy(part, part, og_ss.at[j, k], og_rs.at[j, b], (p, b))

    def own_grad(j):
        total = recon[piece(j, q), :]
        for k in range(1, blocks):
            rs_in(j, k).wait_recv()
            total = total + rsr[blk(k), mine(j)].astype(F32)
        og[piece(j, q), :] = ((total - mlp[mine(j), :].astype(F32)) * rscale).astype(BF16)
        for k in others:
            og_copy(j, k).start()

    def zd_copy(l, j):
        return rcopy(zds.at[l, :, span(j)], zdr.at[l, :, span(j)], zd_ss.at[l, j], zd_rs.at[l, j], down)

    def y_copy(j):
        return rcopy(ys.at[:, span(j)], yr.at[:, span(j)], y_ss.at[j], y_rs.at[j], partner)

    def back(l, j, h):
        return lax.dot_general(
            og[span(j), :], v[l, h * half:(h + 1) * half, :], (((1,), (1,)), ((), ())), preferred_element_type=F32
        )

    def backward(j):
        for k in range(1, blocks):
            og_in(j, k).wait_recv()

        def produce(l):
            for h in range(2):
                acc[l, h, span(j)] = back(l, j, h)

            @pl.when(last)
            def _():
                pass_on(l, j)

        loop(0, t + 1, produce)

    def pass_on(l, j):
        @pl.when(l < t)
        def _():
            for h in range(2):
                zds[l, h, span(j)] = acc[l, h, span(j)].astype(BF16)
            zd_copy(l, j).start()

        @pl.when(l == t)
        def _():
            for h in range(2):
                ys[h, span(j)] = acc[l, h, span(j)].astype(BF16)
            y_copy(j).start()

    def combine(j):
        def add(l):
            zd_copy(l, j).wait_recv()
            for h in range(2):
                acc[l, h, span(j)] += zdr[l, h, span(j)].astype(F32)
            pass_on(l, j)

        loop(0, t + 1, add)

    def masked(j):
        y_copy(j).wait_recv()
        lo_copy(j).wait_recv()
        active = pre[span(j), :] + lor[span(j), :].astype(F32) > 0.0
        for h in range(2):
            total = acc[t, h, span(j)] + yr[h, span(j)].astype(F32)
            side = slice(h * half, (h + 1) * half)
            pg[span(j), side] = jnp.where(active[:, side], total, 0.0).astype(BF16)

    def dec_copy(l):
        return pltpu.make_async_copy(dec.at[l], dec_out.at[l], dec_sem.at[l])

    def dec_piece(l):
        for h in range(2):
            part = lax.dot_general(lat[l, h], og[...], (((0,), (0,)), ((), ())), preferred_element_type=F32)
            dec[l, h * half:(h + 1) * half, :] = part.astype(BF16)
        dec_copy(l).start()

    def blank(l):
        dec[l] = jnp.zeros((2 * half, dec.shape[2]), BF16)
        dec_copy(l).start()

    near = t == top - 1
    grad_lag = jnp.where(last, 1, 2)
    back_lag = jnp.where(last, 1, 3)
    sum_lag = jnp.where(last, 1, jnp.where(near, 3, max(n, 3)))
    dec_at = n + sum_lag - below.astype(jnp.int32)
    v_copy.wait()
    mlp_copy.wait()

    def step(i):
        live = i < n

        @pl.when(i + ahead < n)
        def _():
            encode(i + ahead)

        @pl.when(live)
        def _():
            own_latents(i)

        @pl.when(jnp.logical_and(live, t > 0))
        def _():
            relay(t - 1, i)

        j = i - grad_lag

        @pl.when(jnp.logical_and(j >= 0, j < n))
        def _():
            own_grad(j)

        @pl.when(live)
        def _():
            loop(2, t, lambda d: relay(t - d, i))

        j2 = i - back_lag

        @pl.when(jnp.logical_and(j2 >= 0, j2 < n))
        def _():
            backward(j2)

        @pl.when(jnp.logical_and(live, t > 1))
        def _():
            relay(0, i)

        @pl.when(live)
        def _():
            send_sums(i)

        @pl.when(i == dec_at)
        def _():
            loop(0, t + 1, dec_piece)

        j3 = i - sum_lag

        @pl.when(jnp.logical_and(below, jnp.logical_and(j3 >= 0, j3 < n)))
        def _():
            combine(j3)

        @pl.when(jnp.logical_and(j3 >= 1, j3 <= n))
        def _():
            masked(j3 - 1)

    loop(t + 1, layers, blank)
    loop(0, n + sum_lag + 1, step)

    pg_copy = pltpu.make_async_copy(pg, pg_out, out_sem.at[0])
    xg_copy = pltpu.make_async_copy(xg, xg_out, out_sem.at[1])
    pg_copy.start()
    xg_copy.start()

    def drain(j):
        for k in range(1, blocks):
            x_copy(j, k).wait_send()
            rs_copy(j, k).wait_send()
            og_copy(j, k).wait_send()
        hi_copy(j).wait_send()
        lo_copy(j).wait_send()
        y_copy(j).wait_send()

        def passed(l):
            @pl.when(below)
            def _():
                zu_copy(l, j).wait_send()

            @pl.when(l < t)
            def _():
                zd_copy(l, j).wait_send()

        loop(0, t + 1, passed)

    loop(0, n, drain)
    for l in range(layers):
        dec_copy(l).wait()
    pg_copy.wait()
    xg_copy.wait()


def exchange(layer_inputs, mlp_outputs, enc_weight, enc_bias, dec_weight):
    layers, latents, width = dec_weight.shape
    blocks = lax.axis_size("latent")
    rb, depth = layer_inputs.shape
    rows = rb * blocks
    half = latents // 2
    rscale = rows ** (-0.5)
    chunks = next((c for c in CHUNKS if rb % (16 * c) == 0), 1)
    hbm = pl.BlockSpec(memory_space=pltpu.HBM)
    dma = pltpu.SemaphoreType.DMA
    per_chunk = dma((chunks,))
    per_block = dma((chunks, blocks))
    per_layer = dma((layers, chunks))
    whole = pltpu.VMEM((rows, latents), BF16)
    sides = pltpu.VMEM((2, rows, half), BF16)
    sent = pltpu.VMEM((layers, 2, rows, half), BF16)
    return pl.pallas_call(
        functools.partial(exchange_kernel, layers, blocks, chunks, rscale),
        out_shape=(
            jax.ShapeDtypeStruct((layers, latents, width), BF16),
            jax.ShapeDtypeStruct((rows, depth), BF16),
            jax.ShapeDtypeStruct((rows, latents), BF16),
        ),
        in_specs=[hbm] * 5,
        out_specs=(pl.BlockSpec(memory_space=pl.ANY),) * 3,
        scratch_shapes=[
            pltpu.VMEM((rows, depth), BF16),
            pltpu.VMEM((rb, width), BF16),
            pltpu.VMEM((depth, latents), BF16),
            pltpu.VMEM((layers, latents), F32),
            pltpu.VMEM((layers, latents, width), BF16),
            pltpu.VMEM((rows, latents), F32),
            whole, whole, whole, whole,
            sent,
            pltpu.VMEM((rows, width), F32),
            pltpu.VMEM((rows, width), BF16),
            pltpu.VMEM((blocks, rb, width), BF16),
            pltpu.VMEM((rows, width), BF16),
            pltpu.VMEM((layers, 2, rows, half), F32),
            sent, sent, sides, sides, whole,
            pltpu.VMEM((layers, latents, width), BF16),
            per_block, per_block, per_chunk, per_chunk, per_chunk, per_chunk, per_layer, per_layer,
            per_block, per_block, per_block, per_block, per_layer, per_layer, per_chunk, per_chunk,
            per_chunk, dma((4,)), dma((layers,)), dma((2,)),
        ],
        compiler_params=pltpu.CompilerParams(
            collective_id=0, has_side_effects=True, vmem_limit_bytes=56 * 2**20
        ),
        name="exchange",
    )(layer_inputs, mlp_outputs, enc_weight, enc_bias, dec_weight)


def finish_kernel(
    xg_hbm, pg_hbm, dec_hbm, enc_out, dec_out, xg, pg, enc, dec, in_sem, dec_in, dec_sem, enc_sem
):
    layers = dec.shape[0]
    piece = enc.shape[0] // layers
    ins = [
        pltpu.make_async_copy(xg_hbm, xg, in_sem.at[0]),
        pltpu.make_async_copy(pg_hbm, pg, in_sem.at[1]),
    ]
    reads = [pltpu.make_async_copy(dec_hbm.at[l], dec.at[l], dec_in.at[l]) for l in range(layers)]
    for copy in ins + reads:
        copy.start()
    for copy in ins:
        copy.wait()
    writes = []
    for l in range(layers):
        part = pl.ds(l * piece, piece)
        enc[part, :] = lax.dot_general(
            xg[:, part], pg[...], (((0,), (0,)), ((), ())), preferred_element_type=F32
        )
        writes.append(pltpu.make_async_copy(enc.at[part], enc_out.at[part], enc_sem.at[l]))
        writes[-1].start()
        reads[l].wait()
        writes.append(pltpu.make_async_copy(dec.at[l], dec_out.at[l], dec_sem.at[l]))
        writes[-1].start()
    for copy in writes:
        copy.wait()


def local(layer_inputs, mlp_outputs, enc_weight, enc_bias, dec_weight):
    dec, xg, pg = exchange(layer_inputs, mlp_outputs, enc_weight, enc_bias, dec_weight)
    hbm = pl.BlockSpec(memory_space=pltpu.HBM)
    per_layer = pltpu.SemaphoreType.DMA((dec.shape[0],))
    return pl.pallas_call(
        finish_kernel,
        in_specs=[hbm] * 3,
        out_specs=(hbm,) * 2,
        out_shape=(
            jax.ShapeDtypeStruct(enc_weight.shape, F32),
            jax.ShapeDtypeStruct(dec_weight.shape, BF16),
        ),
        scratch_shapes=[
            pltpu.VMEM(xg.shape, BF16),
            pltpu.VMEM(pg.shape, BF16),
            pltpu.VMEM(enc_weight.shape, F32),
            pltpu.VMEM(dec.shape, BF16),
            pltpu.SemaphoreType.DMA((2,)),
            per_layer, per_layer, per_layer,
        ],
        compiler_params=pltpu.CompilerParams(vmem_limit_bytes=56 * 2**20),
        name="finish",
    )(xg, pg, dec)


def solution(mesh):
    in_specs = (
        P("latent", "layer"),
        P("latent", "layer"),
        P("layer", "latent"),
        P(None, "latent"),
        P(None, "latent", "layer"),
    )
    out_specs = (P("layer", "latent"), P(None, "latent", "layer"))
    return jax.shard_map(local, mesh=mesh, in_specs=in_specs, out_specs=out_specs, check_vma=False)
```

time: 119 us -> 121 us (1.017)
  the two profiles are of different devices: /device:TPU:20 before, /device:TPU:0 now
where the time goes in v1:
time: 121 us
  Pallas kernels  121 us (100%)
    pallas_call x1, Pallas kernels, exchange(): pl.pallas_call(functools.partial(exchange_kernel, layers, blocks, chunks,...  112 us
    pallas_call x1, Pallas kernels, local(): pl.pallas_call(finish_kernel, in_specs=[hbm] * 3, out_specs=(hbm,) * 2, o...  8.4 us

profile of v1, /device:TPU:0, one launch (start us, length us, event | category | flops | bytes accessed | tf_op | source)
XLA Modules:
  0.0 121.2 jit_solution(8936703473044124353)
XLA Ops:
  0.6 112.1 %exchange.1 = (bf16[4,1024,1024]{2,1,0:T(8,128)(2,1)}, bf16[384,1024]{1,0:T(8,128)(2,1)}, bf16[384,1024]{1,0:T(8,128)(2,1)}) custom-call(bf16[96,1024]{1,0:T(8,128)(2,1)} %x_hbm.1, bf16[96,1024]{1,0:T(8,128)(2,1)} %mlp_hbm.1, bf16[1024,1024]{1,0:T(8,128)(2,1)} %w_hbm.1, f32[4,1024]{1,0:T(4,128)} %bias_hbm.1, bf16[4,1024,1024]{2,1,0:T(8,128)(2,1)} %v_hbm.1), custom_call_target="tpu_custom_call" | custom-call | tf_op jit(solution)/shard_map/exchange/pallas_call | solution.py:376
  112.8 8.4 %finish.1 = (f32[1024,1024]{1,0:T(8,128)}, bf16[4,1024,1024]{2,1,0:T(8,128)(2,1)}) custom-call(bf16[384,1024]{1,0:T(8,128)(2,1)} %get-tuple-element.5.xg_hbm, bf16[384,1024]{1,0:T(8,128)(2,1)} %get-tuple-element.6.pg_hbm, bf16[4,1024,1024]{2,1,0:T(8,128)(2,1)} %get-tuple-element.7.dec_hbm), custom_call_target="tpu_custom_call" | custom-call | tf_op jit(solution)/shard_map/finish/pallas_call | solution.py:445

commit v2 on v1

v2 whole, which is shorter than its diff:
```python
import functools

import jax
import jax.numpy as jnp
from jax import lax
from jax.experimental import pallas as pl
from jax.experimental.pallas import tpu as pltpu
from jax.sharding import PartitionSpec as P

MESH = pl.DeviceIdType.MESH
F32 = jnp.float32
BF16 = jnp.bfloat16
CHUNKS = (6, 3, 2)
NEAR = 5


def exchange_kernel(
    layers, blocks, chunks, rscale,
    x_hbm, mlp_hbm, w_hbm, bias_hbm, v_hbm,
    dec, xg, pg,
    mlp, w, bias_all, v, pre, his, hir, los, lor, lat, recon, rss, rsr, og, acc, zds, zdr, ys, yr,
    x_ss, x_rs, hi_ss, hi_rs, lo_ss, lo_rs, zu_ss, zu_rs, rs_ss, rs_rs, og_ss, og_rs, zd_ss, zd_rs, y_ss, y_rs,
    own_sem, in_sem,
):
    p = lax.axis_index("layer")
    q = lax.axis_index("latent")
    t = p // 2
    y = p % 2
    n = chunks
    top = layers - 1
    last = t == top
    below = t < top
    s = x_hbm.shape[0] // n
    size = s * blocks
    half = w.shape[1] // 2
    partner = (p + 1 - 2 * y, q)
    up = (p + 2, q)
    down = (p - 2, q)
    chips = blocks // 2

    def blk(k):
        return ((q // 2 + k // 2) % chips) * 2 + (q % 2 + k % 2) % 2

    def span(j):
        return pl.ds(pl.multiple_of(j * size, size), size)

    def piece(j, b):
        return pl.ds(pl.multiple_of(j * size + b * s, s), s)

    def mine(j):
        return pl.ds(pl.multiple_of(j * s, s), s)

    def rcopy(src, dst, ss, rs, dev):
        return pltpu.make_async_remote_copy(
            src_ref=src, dst_ref=dst, send_sem=ss, recv_sem=rs, device_id=dev, device_id_type=MESH
        )

    def loop(lower, upper, step):
        def body(i, carry):
            step(i)
            return carry

        lax.fori_loop(lower, upper, body, 0)

    def own_x(j):
        return pltpu.make_async_copy(x_hbm.at[mine(j)], xg.at[piece(j, q)], own_sem.at[j])

    w_copy = pltpu.make_async_copy(w_hbm, w, in_sem.at[0])
    bias_copy = pltpu.make_async_copy(bias_hbm, bias_all, in_sem.at[1])
    mlp_copy = pltpu.make_async_copy(mlp_hbm, mlp, in_sem.at[2])
    v_copy = pltpu.make_async_copy(v_hbm, v, in_sem.at[3])
    for j in range(n):
        own_x(j).start()
    for copy in (w_copy, bias_copy, mlp_copy, v_copy):
        copy.start()

    barrier = pltpu.get_barrier_semaphore()
    for k in range(1, blocks):
        pl.semaphore_signal(barrier, inc=1, device_id=(p, blk(k)), device_id_type=MESH)
    pl.semaphore_signal(barrier, inc=1, device_id=partner, device_id_type=MESH)

    @pl.when(below)
    def _():
        pl.semaphore_signal(barrier, inc=1, device_id=up, device_id_type=MESH)

    @pl.when(t > 0)
    def _():
        pl.semaphore_signal(barrier, inc=1, device_id=down, device_id_type=MESH)

    neighbours = blocks + below.astype(jnp.int32) + (t > 0).astype(jnp.int32)
    pl.semaphore_wait(barrier, neighbours)

    others = list(range(2, blocks)) + [1]

    def x_copy(j, k):
        return rcopy(x_hbm.at[mine(j)], xg.at[piece(j, q)], x_ss.at[j, k], x_rs.at[j, q], (p, blk(k)))

    def x_in(j, k):
        b = blk(k)
        return rcopy(x_hbm.at[mine(j)], xg.at[piece(j, b)], x_ss.at[j, k], x_rs.at[j, b], (p, b))

    def send_x(j):
        for k in others:
            x_copy(j, k).start()

    loop(0, n, send_x)

    def side(h):
        return slice(h * half, (h + 1) * half)

    def hi_copy(j, h):
        return rcopy(his.at[h, span(j)], hir.at[h, span(j)], hi_ss.at[j, h], hi_rs.at[j, h], partner)

    def lo_copy(j):
        return rcopy(los.at[:, span(j)], lor.at[:, span(j)], lo_ss.at[j], lo_rs.at[j], partner)

    def encode(j):
        own_x(j).wait()
        for k in others:
            x_in(j, k).wait_recv()
        for h in range(2):
            part = jnp.dot(xg[span(j), :], w[:, side(h)], preferred_element_type=F32)
            pre[h, span(j)] = part
            hi = part.astype(BF16)
            his[h, span(j)] = hi
            hi_copy(j, h).start()
            los[h, span(j)] = (part - hi.astype(F32)).astype(BF16)

    def zu_copy(l, j, h):
        part = lat.at[l, h, span(j)]
        return rcopy(part, part, zu_ss.at[l, j, h], zu_rs.at[l, j, h], up)

    bias_copy.wait()
    own_row = lax.broadcasted_iota(jnp.int32, bias_all.shape, 0) == t
    bias = jnp.sum(jnp.where(own_row, bias_all[...], 0.0), axis=0, keepdims=True)
    w_copy.wait()
    ahead = min(n, 3)
    early = min(n, 2)
    loop(0, early, encode)

    def decoded(l, j):
        return jnp.dot(lat[l, 0, span(j)], v[l, :half, :], preferred_element_type=F32) + jnp.dot(
            lat[l, 1, span(j)], v[l, half:, :], preferred_element_type=F32
        )

    def own_latents(j):
        for h in range(2):
            hi_copy(j, h).wait_recv()
            total = pre[h, span(j)] + hir[h, span(j)].astype(F32) + bias[:, side(h)]
            pre[h, span(j)] = total
            lat[t, h, span(j)] = jnp.maximum(total, 0.0).astype(BF16)

            @pl.when(below)
            def _():
                zu_copy(t, j, h).start()

        lo_copy(j).start()

    def relay(l, j):
        for h in range(2):
            zu_copy(l, j, h).wait_recv()

            @pl.when(below)
            def _():
                zu_copy(l, j, h).start()

        recon[span(j), :] += decoded(l, j)

    def rs_copy(j, k):
        b = blk(k)
        return rcopy(rss.at[piece(j, b)], rsr.at[q, mine(j)], rs_ss.at[j, k], rs_rs.at[j, q], (p, b))

    def rs_in(j, k):
        b = blk(k)
        return rcopy(rss.at[piece(j, b)], rsr.at[b, mine(j)], rs_ss.at[j, k], rs_rs.at[j, b], (p, b))

    def send_sums(j):
        rss[span(j), :] = recon[span(j), :].astype(BF16)
        for k in others:
            rs_copy(j, k).start()

    def og_copy(j, k):
        part = og.at[piece(j, q)]
        return rcopy(part, part, og_ss.at[j, k], og_rs.at[j, q], (p, blk(k)))

    def og_in(j, k):
        b = blk(k)
        part = og.at[piece(j, b)]
        return rcopy(part, part, og_ss.at[j, k], og_rs.at[j, b], (p, b))

    def own_grad(j):
        total = recon[piece(j, q), :]
        for k in range(1, blocks):
            rs_in(j, k).wait_recv()
            total = total + rsr[blk(k), mine(j)].astype(F32)
        og[piece(j, q), :] = ((total - mlp[mine(j), :].astype(F32)) * rscale).astype(BF16)
        for k in others:
            og_copy(j, k).start()

    def zd_copy(l, j, h):
        return rcopy(zds.at[l, h, span(j)], zdr.at[l, h, span(j)], zd_ss.at[l, j, h], zd_rs.at[l, j, h], down)

    def y_copy(j, h):
        return rcopy(ys.at[h, span(j)], yr.at[h, span(j)], y_ss.at[j, h], y_rs.at[j, h], partner)

    def back(l, j, h):
        return lax.dot_general(
            og[span(j), :], v[l, h * half:(h + 1) * half, :], (((1,), (1,)), ((), ())), preferred_element_type=F32
        )

    def backward(j):
        for k in range(1, blocks):
            og_in(j, k).wait_recv()

        def produce(l):
            for h in range(2):
                acc[l, h, span(j)] = back(l, j, h)

                @pl.when(last)
                def _():
                    pass_on(l, j, h)

        loop(0, t + 1, produce)

    def pass_on(l, j, h):
        @pl.when(l < t)
        def _():
            zds[l, h, span(j)] = acc[l, h, span(j)].astype(BF16)
            zd_copy(l, j, h).start()

        @pl.when(l == t)
        def _():
            ys[h, span(j)] = acc[l, h, span(j)].astype(BF16)
            y_copy(j, h).start()

    def combine(j):
        def add(l):
            for h in range(2):
                zd_copy(l, j, h).wait_recv()
                acc[l, h, span(j)] += zdr[l, h, span(j)].astype(F32)
                pass_on(l, j, h)

            @pl.when(j == n - 1)
            def _():
                dec_piece(l)

        loop(0, t + 1, add)

    def masked(j):
        lo_copy(j).wait_recv()
        for h in range(2):
            y_copy(j, h).wait_recv()
            active = pre[h, span(j)] + lor[h, span(j)].astype(F32) > 0.0
            total = acc[t, h, span(j)] + yr[h, span(j)].astype(F32)
            pg[span(j), side(h)] = jnp.where(active, total, 0.0).astype(BF16)

    def dec_piece(l):
        for h in range(2):
            part = lax.dot_general(lat[l, h], og[...], (((0,), (0,)), ((), ())), preferred_element_type=F32)
            dec[l, h * half:(h + 1) * half, :] = part.astype(BF16)

    def blank(l):
        dec[l] = jnp.zeros((2 * half, dec.shape[2]), BF16)

    near = t == top - 1
    grad_lag = jnp.where(last, 1, 2)
    back_lag = jnp.where(last, 1, 3)
    sum_lag = jnp.where(last, 1, jnp.where(near, NEAR, max(n, NEAR)))
    own_latents(0)
    loop(early, ahead, encode)
    v_copy.wait()
    mlp_copy.wait()

    def step(i):
        live = i < n

        @pl.when(i + 1 < n)
        def _():
            own_latents(i + 1)

        @pl.when(i + ahead < n)
        def _():
            encode(i + ahead)

        @pl.when(live)
        def _():
            recon[span(i), :] = decoded(t, i)

        @pl.when(jnp.logical_and(live, t > 0))
        def _():
            relay(t - 1, i)

        j = i - grad_lag

        @pl.when(jnp.logical_and(j >= 0, j < n))
        def _():
            own_grad(j)

        @pl.when(live)
        def _():
            loop(2, t, lambda d: relay(t - d, i))

        @pl.when(jnp.logical_and(live, t > 1))
        def _():
            relay(0, i)

        @pl.when(live)
        def _():
            send_sums(i)

        j2 = i - back_lag

        @pl.when(jnp.logical_and(j2 >= 0, j2 < n))
        def _():
            backward(j2)

        @pl.when(jnp.logical_and(last, i == n + sum_lag))
        def _():
            loop(0, t + 1, dec_piece)

        j3 = i - sum_lag

        @pl.when(jnp.logical_and(below, jnp.logical_and(j3 >= 0, j3 < n)))
        def _():
            combine(j3)

        @pl.when(jnp.logical_and(j3 >= 1, j3 <= n))
        def _():
            masked(j3 - 1)

    loop(t + 1, layers, blank)
    loop(0, n + sum_lag + 1, step)

    def drain(j):
        for k in range(1, blocks):
            x_copy(j, k).wait_send()
            rs_copy(j, k).wait_send()
            og_copy(j, k).wait_send()
        lo_copy(j).wait_send()
        for h in range(2):
            hi_copy(j, h).wait_send()
            y_copy(j, h).wait_send()

        def passed(l):
            @pl.when(below)
            def _():
                for h in range(2):
                    zu_copy(l, j, h).wait_send()

            @pl.when(l < t)
            def _():
                for h in range(2):
                    zd_copy(l, j, h).wait_send()

        loop(0, t + 1, passed)

    loop(0, n, drain)


def exchange(layer_inputs, mlp_outputs, enc_weight, enc_bias, dec_weight):
    layers, latents, width = dec_weight.shape
    blocks = lax.axis_size("latent")
    rb, depth = layer_inputs.shape
    rows = rb * blocks
    half = latents // 2
    rscale = rows ** (-0.5)
    chunks = next((c for c in CHUNKS if rb % (16 * c) == 0), 1)
    hbm = pl.BlockSpec(memory_space=pltpu.HBM)
    dma = pltpu.SemaphoreType.DMA
    per_chunk = dma((chunks,))
    per_block = dma((chunks, blocks))
    per_layer = dma((layers, chunks, 2))
    per_side = dma((chunks, 2))
    sides = pltpu.VMEM((2, rows, half), BF16)
    sent = pltpu.VMEM((layers, 2, rows, half), BF16)
    return pl.pallas_call(
        functools.partial(exchange_kernel, layers, blocks, chunks, rscale),
        out_shape=(
            pltpu.VMEM((layers, latents, width), BF16),
            pltpu.VMEM((rows, depth), BF16),
            pltpu.VMEM((rows, latents), BF16),
        ),
        in_specs=[hbm] * 5,
        out_specs=(pl.BlockSpec(memory_space=pltpu.VMEM),) * 3,
        scratch_shapes=[
            pltpu.VMEM((rb, width), BF16),
            pltpu.VMEM((depth, latents), BF16),
            pltpu.VMEM((layers, latents), F32),
            pltpu.VMEM((layers, latents, width), BF16),
            pltpu.VMEM((2, rows, half), F32),
            sides, sides, sides, sides,
            sent,
            pltpu.VMEM((rows, width), F32),
            pltpu.VMEM((rows, width), BF16),
            pltpu.VMEM((blocks, rb, width), BF16),
            pltpu.VMEM((rows, width), BF16),
            pltpu.VMEM((layers, 2, rows, half), F32),
            sent, sent, sides, sides,
            per_block, per_block, per_side, per_side, per_chunk, per_chunk, per_layer, per_layer,
            per_block, per_block, per_block, per_block, per_layer, per_layer, per_side, per_side,
            per_chunk, dma((4,)),
        ],
        compiler_params=pltpu.CompilerParams(
            collective_id=0, has_side_effects=True, vmem_limit_bytes=40 * 2**20
        ),
        name="exchange",
    )(*(pltpu.with_memory_space_constraint(a, pltpu.HBM) for a in (layer_inputs, mlp_outputs, enc_weight, enc_bias, dec_weight)))


def finish_kernel(xg, pg, dec, enc_out, dec_out, enc, enc_sem, dec_sem):
    layers = dec.shape[0]
    piece = enc.shape[0] // layers
    writes = [pltpu.make_async_copy(dec.at[l], dec_out.at[l], dec_sem.at[l]) for l in range(layers)]
    for copy in writes:
        copy.start()
    for l in range(layers):
        part = pl.ds(l * piece, piece)
        enc[part, :] = lax.dot_general(
            xg[:, part], pg[...], (((0,), (0,)), ((), ())), preferred_element_type=F32
        )
        writes.append(pltpu.make_async_copy(enc.at[part], enc_out.at[part], enc_sem.at[l]))
        writes[-1].start()
    for copy in writes:
        copy.wait()


def local(layer_inputs, mlp_outputs, enc_weight, enc_bias, dec_weight):
    dec, xg, pg = exchange(layer_inputs, mlp_outputs, enc_weight, enc_bias, dec_weight)
    hbm = pl.BlockSpec(memory_space=pltpu.HBM)
    per_layer = pltpu.SemaphoreType.DMA((dec.shape[0],))
    return pl.pallas_call(
        finish_kernel,
        in_specs=[pl.BlockSpec(memory_space=pltpu.VMEM)] * 3,
        out_specs=(hbm,) * 2,
        out_shape=(
            jax.ShapeDtypeStruct(enc_weight.shape, F32),
            jax.ShapeDtypeStruct(dec_weight.shape, BF16),
        ),
        scratch_shapes=[pltpu.VMEM(enc_weight.shape, F32), per_layer, per_layer],
        compiler_params=pltpu.CompilerParams(vmem_limit_bytes=24 * 2**20),
        name="finish",
    )(xg, pg, dec)


def solution(mesh):
    in_specs = (
        P("latent", "layer"),
        P("latent", "layer"),
        P("layer", "latent"),
        P(None, "latent"),
        P(None, "latent", "layer"),
    )
    out_specs = (P("layer", "latent"), P(None, "latent", "layer"))
    return jax.shard_map(local, mesh=mesh, in_specs=in_specs, out_specs=out_specs, check_vma=False)
```

time: 121 us -> 103 us (0.85)
  Pallas kernels: 121 us -> 102 us
    pallas_call x1, Pallas kernels: 112 us -> 97.7 us  [exchange(): pl.pallas_call(functools.partial(exchange_kernel, layers, blocks, chunks,...]
    pallas_call x1, Pallas kernels: 8.4 us -> 4.63 us  [local(): pl.pallas_call(finish_kernel, in_specs=[pl.BlockSpec(memory_space=pltpu.V...]
where the time goes in v2:
time: 103 us
  Pallas kernels  102 us (99%)
    pallas_call x1, Pallas kernels, exchange(): pl.pallas_call(functools.partial(exchange_kernel, layers, blocks, chunks,...  97.7 us
    pallas_call x1, Pallas kernels, local(): pl.pallas_call(finish_kernel, in_specs=[pl.BlockSpec(memory_space=pltpu.V...  4.63 us

profile of v2, /device:TPU:0, one launch (start us, length us, event | category | flops | bytes accessed | tf_op | source)
XLA Modules:
  0.0 103.0 jit_solution(1472719051668246142)
XLA Ops:
  0.6 97.7 %exchange.1 = (bf16[4,1024,1024]{2,1,0:T(8,128)(2,1)S(1)}, bf16[384,1024]{1,0:T(8,128)(2,1)S(1)}, bf16[384,1024]{1,0:T(8,128)(2,1)S(1)}) custom-call(bf16[96,1024]{1,0:T(8,128)(2,1)} %x_hbm.1, bf16[96,1024]{1,0:T(8,128)(2,1)} %mlp_hbm.1, bf16[1024,1024]{1,0:T(8,128)(2,1)} %w_hbm.1, f32[4,1024]{1,0:T(4,128)} %bias_hbm.1, bf16[4,1024,1024]{2,1,0:T(8,128)(2,1)} %v_hbm.1), custom_call_target="tpu_custom_call" | custom-call | tf_op jit(solution)/shard_map/exchange/pallas_call | solution.py:376
  98.4 4.6 %finish.1 = (f32[1024,1024]{1,0:T(8,128)}, bf16[4,1024,1024]{2,1,0:T(8,128)(2,1)}) custom-call(bf16[384,1024]{1,0:T(8,128)(2,1)S(1)} %get-tuple-element.5.xg, bf16[384,1024]{1,0:T(8,128)(2,1)S(1)} %get-tuple-element.6.pg, bf16[4,1024,1024]{2,1,0:T(8,128)(2,1)S(1)} %get-tuple-element.7.dec), custom_call_target="tpu_custom_call" | custom-call | tf_op jit(solution)/shard_map/finish/pallas_call | solution.py:431

commit v3 on v2

--- a/solution.py
+++ b/solution.py
@@ -11,16 +11,18 @@
 F32 = jnp.float32
 BF16 = jnp.bfloat16
 CHUNKS = (6, 3, 2)
-NEAR = 5
+NEAR = 4
+FROM = 1
+SWAPS = 2
 
 
 def exchange_kernel(
     layers, blocks, chunks, rscale,
     x_hbm, mlp_hbm, w_hbm, bias_hbm, v_hbm,
     dec, xg, pg,
-    mlp, w, bias_all, v, pre, his, hir, los, lor, lat, recon, rss, rsr, og, acc, zds, zdr, ys, yr,
+    mlp, w, bias_all, v, pre, his, hir, los, lor, lat, recon, rss, rsr, og, acc, zds, zdr, ys, yr, bss, bsr,
     x_ss, x_rs, hi_ss, hi_rs, lo_ss, lo_rs, zu_ss, zu_rs, rs_ss, rs_rs, og_ss, og_rs, zd_ss, zd_rs, y_ss, y_rs,
-    own_sem, in_sem,
+    fs_ss, fs_rs, bs_ss, bs_rs, own_sem, in_sem,
 ):
     p = lax.axis_index("layer")
     q = lax.axis_index("latent")
@@ -30,6 +32,7 @@
     top = layers - 1
     last = t == top
     below = t < top
+    near = t == top - 1
     s = x_hbm.shape[0] // n
     size = s * blocks
     half = w.shape[1] // 2
@@ -37,6 +40,7 @@
     up = (p + 2, q)
     down = (p - 2, q)
     chips = blocks // 2
+    other = 1 - y
 
     def blk(k):
         return ((q // 2 + k // 2) % chips) * 2 + (q % 2 + k % 2) % 2
@@ -62,8 +66,11 @@
 
         lax.fori_loop(lower, upper, body, 0)
 
+    def settle(ref, sem):
+        pltpu.make_async_copy(ref, ref, sem).wait()
+
     def own_x(j):
-        return pltpu.make_async_copy(x_hbm.at[mine(j)], xg.at[piece(j, q)], own_sem.at[j])
+        return pltpu.make_async_copy(x_hbm.at[mine(j)], xg.at[piece(j, q)], own_sem)
 
     w_copy = pltpu.make_async_copy(w_hbm, w, in_sem.at[0])
     bias_copy = pltpu.make_async_copy(bias_hbm, bias_all, in_sem.at[1])
@@ -93,31 +100,32 @@
     others = list(range(2, blocks)) + [1]
 
     def x_copy(j, k):
-        return rcopy(x_hbm.at[mine(j)], xg.at[piece(j, q)], x_ss.at[j, k], x_rs.at[j, q], (p, blk(k)))
-
-    def x_in(j, k):
-        b = blk(k)
-        return rcopy(x_hbm.at[mine(j)], xg.at[piece(j, b)], x_ss.at[j, k], x_rs.at[j, b], (p, b))
+        part = xg.at[piece(j, q)]
+        return rcopy(part, part, x_ss, x_rs.at[j], (p, blk(k)))
 
     def send_x(j):
         for k in others:
             x_copy(j, k).start()
 
+    arrivals = pl.ds(0, (blocks - 1) * s)
+    departures = pl.ds(0, (blocks - 1) * s * n)
+    settle(xg.at[pl.ds(0, s * n)], own_sem)
     loop(0, n, send_x)
+
+    def part_of(h):
+        return pl.ds(pl.multiple_of(h * half, half), half)
 
     def side(h):
         return slice(h * half, (h + 1) * half)
 
     def hi_copy(j, h):
-        return rcopy(his.at[h, span(j)], hir.at[h, span(j)], hi_ss.at[j, h], hi_rs.at[j, h], partner)
+        return rcopy(his.at[h, span(j)], hir.at[h, span(j)], hi_ss, hi_rs.at[j, h], partner)
 
     def lo_copy(j):
-        return rcopy(los.at[:, span(j)], lor.at[:, span(j)], lo_ss.at[j], lo_rs.at[j], partner)
+        return rcopy(los.at[:, span(j)], lor.at[:, span(j)], lo_ss, lo_rs.at[j], partner)
 
     def encode(j):
-        own_x(j).wait()
-        for k in others:
-            x_in(j, k).wait_recv()
+        settle(xg.at[arrivals], x_rs.at[j])
         for h in range(2):
             part = jnp.dot(xg[span(j), :], w[:, side(h)], preferred_element_type=F32)
             pre[h, span(j)] = part
@@ -128,13 +136,13 @@
 
     def zu_copy(l, j, h):
         part = lat.at[l, h, span(j)]
-        return rcopy(part, part, zu_ss.at[l, j, h], zu_rs.at[l, j, h], up)
+        return rcopy(part, part, zu_ss.at[l, h], zu_rs.at[l, j, h], up)
 
     bias_copy.wait()
     own_row = lax.broadcasted_iota(jnp.int32, bias_all.shape, 0) == t
     bias = jnp.sum(jnp.where(own_row, bias_all[...], 0.0), axis=0, keepdims=True)
     w_copy.wait()
-    ahead = min(n, 3)
+    ahead = jnp.where(last, n, min(n, 3))
     early = min(n, 2)
     loop(0, early, encode)
 
@@ -143,6 +151,12 @@
             lat[l, 1, span(j)], v[l, half:, :], preferred_element_type=F32
         )
 
+    def swapped(l, j):
+        return jnp.logical_and(l == top - 1, jnp.logical_and(j >= FROM, j < FROM + SWAPS))
+
+    def goes_up(l, j, h):
+        return jnp.logical_and(below, jnp.logical_or(jnp.logical_not(swapped(l, j)), y == h))
+
     def own_latents(j):
         for h in range(2):
             hi_copy(j, h).wait_recv()
@@ -150,29 +164,43 @@
             pre[h, span(j)] = total
             lat[t, h, span(j)] = jnp.maximum(total, 0.0).astype(BF16)
 
+            @pl.when(goes_up(t, j, h))
+            def _():
+                zu_copy(t, j, h).start()
+
+        @pl.when(below)
+        def _():
+            lo_copy(j).start()
+
+    def relay(l, j):
+        for h in range(2):
+            zu_copy(l, j, h).wait_recv()
+
             @pl.when(below)
             def _():
-                zu_copy(t, j, h).start()
-
-        lo_copy(j).start()
-
-    def relay(l, j):
-        for h in range(2):
-            zu_copy(l, j, h).wait_recv()
-
-            @pl.when(below)
-            def _():
                 zu_copy(l, j, h).start()
 
         recon[span(j), :] += decoded(l, j)
+
+    def fs_copy(j, h):
+        part = lat.at[top - 1, h, span(j)]
+        return rcopy(part, part, fs_ss, fs_rs.at[j], partner)
+
+    def add_half(j, h):
+        recon[span(j), :] += jnp.dot(lat[top - 1, h, span(j)], v[top - 1, part_of(h), :], preferred_element_type=F32)
+
+    def swap_half(j):
+        zu_copy(top - 1, j, y).wait_recv()
+        fs_copy(j, y).start()
+        add_half(j, y)
+
+    def relay_other(j):
+        fs_copy(j, other).wait_recv()
+        add_half(j, other)
 
     def rs_copy(j, k):
         b = blk(k)
-        return rcopy(rss.at[piece(j, b)], rsr.at[q, mine(j)], rs_ss.at[j, k], rs_rs.at[j, q], (p, b))
-
-    def rs_in(j, k):
-        b = blk(k)
-        return rcopy(rss.at[piece(j, b)], rsr.at[b, mine(j)], rs_ss.at[j, k], rs_rs.at[j, b], (p, b))
+        return rcopy(rss.at[piece(j, b)], rsr.at[q, mine(j)], rs_ss, rs_rs.at[j], (p, b))
 
     def send_sums(j):
         rss[span(j), :] = recon[span(j), :].astype(BF16)
@@ -181,70 +209,111 @@
 
     def og_copy(j, k):
         part = og.at[piece(j, q)]
-        return rcopy(part, part, og_ss.at[j, k], og_rs.at[j, q], (p, blk(k)))
-
-    def og_in(j, k):
-        b = blk(k)
-        part = og.at[piece(j, b)]
-        return rcopy(part, part, og_ss.at[j, k], og_rs.at[j, b], (p, b))
+        return rcopy(part, part, og_ss, og_rs.at[j], (p, blk(k)))
 
     def own_grad(j):
         total = recon[piece(j, q), :]
+        settle(rss.at[arrivals], rs_rs.at[j])
         for k in range(1, blocks):
-            rs_in(j, k).wait_recv()
             total = total + rsr[blk(k), mine(j)].astype(F32)
         og[piece(j, q), :] = ((total - mlp[mine(j), :].astype(F32)) * rscale).astype(BF16)
         for k in others:
             og_copy(j, k).start()
 
     def zd_copy(l, j, h):
-        return rcopy(zds.at[l, h, span(j)], zdr.at[l, h, span(j)], zd_ss.at[l, j, h], zd_rs.at[l, j, h], down)
+        return rcopy(zds.at[l, h, span(j)], zdr.at[l, h, span(j)], zd_ss.at[l, h], zd_rs.at[l, j, h], down)
 
     def y_copy(j, h):
-        return rcopy(ys.at[h, span(j)], yr.at[h, span(j)], y_ss.at[j, h], y_rs.at[j, h], partner)
+        return rcopy(ys.at[h, span(j)], yr.at[h, span(j)], y_ss, y_rs.at[j, h], partner)
+
+    def bs_copy(j):
+        return rcopy(bss.at[span(j)], bsr.at[span(j)], bs_ss, bs_rs.at[j], partner)
 
     def back(l, j, h):
         return lax.dot_general(
-            og[span(j), :], v[l, h * half:(h + 1) * half, :], (((1,), (1,)), ((), ())), preferred_element_type=F32
+            og[span(j), :], v[l, part_of(h), :], (((1,), (1,)), ((), ())), preferred_element_type=F32
         )
 
+    def send_down(l, j, h, total):
+        zds[l, h, span(j)] = total.astype(BF16)
+        zd_copy(l, j, h).start()
+
+    def send_across(j, h, total):
+        acc[t, h, span(j)] = total
+        ys[h, span(j)] = total.astype(BF16)
+        y_copy(j, h).start()
+
+    def send_own(j):
+        for h in range(2):
+            ys[h, span(j)] = acc[top, h, span(j)].astype(BF16)
+            y_copy(j, h).start()
+
     def backward(j):
-        for k in range(1, blocks):
-            og_in(j, k).wait_recv()
-
-        def produce(l):
+        settle(og.at[arrivals], og_rs.at[j])
+
+        @pl.when(last)
+        def _():
+            bss[span(j)] = back(top - 1, j, other).astype(BF16)
+            bs_copy(j).start()
+
+            @pl.when(j > 0)
+            def _():
+                send_own(j - 1)
+
+            def produce(l):
+                for h in range(2):
+                    send_down(l, j, h, back(l, j, h))
+
+            loop(0, top - 1, produce)
             for h in range(2):
-                acc[l, h, span(j)] = back(l, j, h)
-
-                @pl.when(last)
-                def _():
-                    pass_on(l, j, h)
-
-        loop(0, t + 1, produce)
-
-    def pass_on(l, j, h):
-        @pl.when(l < t)
-        def _():
-            zds[l, h, span(j)] = acc[l, h, span(j)].astype(BF16)
-            zd_copy(l, j, h).start()
-
-        @pl.when(l == t)
-        def _():
-            ys[h, span(j)] = acc[l, h, span(j)].astype(BF16)
-            y_copy(j, h).start()
-
-    def combine(j):
+                acc[top, h, span(j)] = back(top, j, h)
+            acc[top - 1, y, span(j)] = back(top - 1, j, y)
+
+            @pl.when(j == n - 1)
+            def _():
+                send_own(j)
+
+        @pl.when(below)
+        def _():
+            def keep(l):
+                for h in range(2):
+                    acc[l, h, span(j)] = back(l, j, h)
+
+            loop(0, t + 1, keep)
+
+    def finish_swap(j):
+        bs_copy(j).wait_recv()
+        send_down(top - 1, j, y, acc[top - 1, y, span(j)] + bsr[span(j)].astype(F32))
+
+    def summed(l, j, h):
+        zd_copy(l, j, h).wait_recv()
+        return acc[l, h, span(j)] + zdr[l, h, span(j)].astype(F32)
+
+    def pass_on(j):
         def add(l):
             for h in range(2):
-                zd_copy(l, j, h).wait_recv()
-                acc[l, h, span(j)] += zdr[l, h, span(j)].astype(F32)
-                pass_on(l, j, h)
+                send_down(l, j, h, summed(l, j, h))
 
             @pl.when(j == n - 1)
             def _():
                 dec_piece(l)
 
-        loop(0, t + 1, add)
+        loop(0, t, add)
+
+    def combine(j):
+        @pl.when(near)
+        def _():
+            send_across(j, other, acc[t, other, span(j)])
+            send_across(j, y, summed(t, j, y))
+
+        @pl.when(jnp.logical_not(near))
+        def _():
+            for h in range(2):
+                send_across(j, h, summed(t, j, h))
+
+        @pl.when(j == n - 1)
+        def _():
+            dec_piece(t)
 
     def masked(j):
         lo_copy(j).wait_recv()
@@ -262,7 +331,6 @@
     def blank(l):
         dec[l] = jnp.zeros((2 * half, dec.shape[2]), BF16)
 
-    near = t == top - 1
     grad_lag = jnp.where(last, 1, 2)
     back_lag = jnp.where(last, 1, 3)
     sum_lag = jnp.where(last, 1, jnp.where(near, NEAR, max(n, NEAR)))
@@ -273,6 +341,12 @@
 
     def step(i):
         live = i < n
+        j = i - grad_lag
+        soon = jnp.logical_and(last, j == n - 1)
+
+        @pl.when(jnp.logical_and(jnp.logical_and(j >= 0, j < n), jnp.logical_not(soon)))
+        def _():
+            own_grad(j)
 
         @pl.when(i + 1 < n)
         def _():
@@ -286,35 +360,60 @@
         def _():
             recon[span(i), :] = decoded(t, i)
 
-        @pl.when(jnp.logical_and(live, t > 0))
+        apart = jnp.logical_and(last, swapped(t - 1, i))
+
+        @pl.when(jnp.logical_and(live, jnp.logical_and(t > 0, jnp.logical_not(apart))))
         def _():
             relay(t - 1, i)
 
-        j = i - grad_lag
-
-        @pl.when(jnp.logical_and(j >= 0, j < n))
-        def _():
-            own_grad(j)
+        @pl.when(jnp.logical_and(live, apart))
+        def _():
+            swap_half(i)
+
+        @pl.when(jnp.logical_and(last, jnp.logical_and(i >= 1, i < n + 1)))
+        def _():
+            lo_copy(i - 1).start()
+
+        @pl.when(jnp.logical_and(last, jnp.logical_and(i >= 2, i < n)))
+        def _():
+            finish_swap(i - 2)
 
         @pl.when(live)
         def _():
             loop(2, t, lambda d: relay(t - d, i))
 
+        j2 = i - back_lag
+        first = jnp.logical_and(last, jnp.logical_and(j2 == 0, n > 1))
+
+        @pl.when(first)
+        def _():
+            backward(j2)
+
         @pl.when(jnp.logical_and(live, t > 1))
         def _():
             relay(0, i)
 
+        @pl.when(jnp.logical_and(live, apart))
+        def _():
+            relay_other(i)
+
         @pl.when(live)
         def _():
             send_sums(i)
 
-        j2 = i - back_lag
-
-        @pl.when(jnp.logical_and(j2 >= 0, j2 < n))
+        @pl.when(jnp.logical_and(last, i == n - 1))
+        def _():
+            own_grad(i)
+
+        @pl.when(jnp.logical_and(jnp.logical_and(j2 >= 0, j2 < n), jnp.logical_not(first)))
         def _():
             backward(j2)
 
-        @pl.when(jnp.logical_and(last, i == n + sum_lag))
+        @pl.when(jnp.logical_and(last, i == n))
+        def _():
+            loop(max(n - 2, 0), n, finish_swap)
+
+        @pl.when(jnp.logical_and(last, i == n + sum_lag + 1))
         def _():
             loop(0, t + 1, dec_piece)
 
@@ -322,39 +421,48 @@
 
         @pl.when(jnp.logical_and(below, jnp.logical_and(j3 >= 0, j3 < n)))
         def _():
-            combine(j3)
-
-        @pl.when(jnp.logical_and(j3 >= 1, j3 <= n))
-        def _():
-            masked(j3 - 1)
+            pass_on(j3)
+
+        @pl.when(jnp.logical_and(below, jnp.logical_and(j3 >= 1, j3 <= n)))
+        def _():
+            combine(j3 - 1)
+
+        @pl.when(jnp.logical_and(j3 >= 2, j3 <= n + 1))
+        def _():
+            masked(j3 - 2)
 
     loop(t + 1, layers, blank)
-    loop(0, n + sum_lag + 1, step)
-
-    def drain(j):
-        for k in range(1, blocks):
-            x_copy(j, k).wait_send()
-            rs_copy(j, k).wait_send()
-            og_copy(j, k).wait_send()
-        lo_copy(j).wait_send()
-        for h in range(2):
-            hi_copy(j, h).wait_send()
-            y_copy(j, h).wait_send()
-
-        def passed(l):
-            @pl.when(below)
-            def _():
-                for h in range(2):
-                    zu_copy(l, j, h).wait_send()
-
-            @pl.when(l < t)
-            def _():
-                for h in range(2):
-                    zd_copy(l, j, h).wait_send()
-
-        loop(0, t + 1, passed)
-
-    loop(0, n, drain)
+    loop(0, n + sum_lag + 2, step)
+
+    for ref, sem in ((xg, x_ss), (rss, rs_ss), (og, og_ss)):
+        settle(ref.at[departures], sem)
+    for ref, sem in ((his, hi_ss), (los, lo_ss), (ys, y_ss)):
+        settle(ref, sem)
+    apart_rows = size * len(range(FROM, min(FROM + SWAPS, n)))
+
+    @pl.when(last)
+    def _():
+        settle(bss, bs_ss)
+        if apart_rows:
+            settle(bss.at[pl.ds(0, apart_rows)], fs_ss)
+
+    def drain(l):
+        for h in range(2):
+            less = jnp.logical_and(l == top - 1, y != h)
+
+            @pl.when(jnp.logical_and(below, jnp.logical_not(less)))
+            def _():
+                settle(lat.at[l, h], zu_ss.at[l, h])
+
+            @pl.when(jnp.logical_and(below, less))
+            def _():
+                settle(lat.at[l, h, pl.ds(0, size * n - apart_rows)], zu_ss.at[l, h])
+
+            @pl.when(jnp.logical_and(l < t, jnp.logical_not(less)))
+            def _():
+                settle(zds.at[l, h], zd_ss.at[l, h])
+
+    loop(0, t + 1, drain)
 
 
 def exchange(layer_inputs, mlp_outputs, enc_weight, enc_bias, dec_weight):
@@ -368,8 +476,9 @@
     hbm = pl.BlockSpec(memory_space=pltpu.HBM)
     dma = pltpu.SemaphoreType.DMA
     per_chunk = dma((chunks,))
-    per_block = dma((chunks, blocks))
-    per_layer = dma((layers, chunks, 2))
+    one = dma
+    per_layer = dma((layers - 1, chunks, 2))
+    sides_sent = dma((layers - 1, 2))
     per_side = dma((chunks, 2))
     sides = pltpu.VMEM((2, rows, half), BF16)
     sent = pltpu.VMEM((layers, 2, rows, half), BF16)
@@ -396,9 +505,10 @@
             pltpu.VMEM((rows, width), BF16),
             pltpu.VMEM((layers, 2, rows, half), F32),
             sent, sent, sides, sides,
-            per_block, per_block, per_side, per_side, per_chunk, per_chunk, per_layer, per_layer,
-            per_block, per_block, per_block, per_block, per_layer, per_layer, per_side, per_side,
-            per_chunk, dma((4,)),
+            pltpu.VMEM((rows, half), BF16), pltpu.VMEM((rows, half), BF16),
+            one, per_chunk, one, per_side, one, per_chunk, sides_sent, per_layer,
+            one, per_chunk, one, per_chunk, sides_sent, per_layer, one, per_side,
+            one, per_chunk, one, per_chunk, one, dma((4,)),
         ],
         compiler_params=pltpu.CompilerParams(
             collective_id=0, has_side_effects=True, vmem_limit_bytes=40 * 2**20

time: 103 us -> 97.1 us (0.943)
  Pallas kernels: 102 us -> 96.3 us
    pallas_call x1, Pallas kernels: 97.7 us -> 91.7 us  [exchange(): pl.pallas_call(functools.partial(exchange_kernel, layers, blocks, chunks,...]
where the time goes in v3:
time: 97.1 us; the launch traced here: 96.9 us
  Pallas kernels  96.3 us (99%)
    pallas_call x1, Pallas kernels, exchange(): pl.pallas_call(functools.partial(exchange_kernel, layers, blocks, chunks,...  91.7 us
    pallas_call x1, Pallas kernels, local(): pl.pallas_call(finish_kernel, in_specs=[pl.BlockSpec(memory_space=pltpu.V...  4.63 us

profile of v3, /device:TPU:0, one launch (start us, length us, event | category | flops | bytes accessed | tf_op | source)
XLA Modules:
  0.0 96.9 jit_solution(14501262389812483087)
XLA Ops:
  0.6 91.7 %exchange.1 = (bf16[4,1024,1024]{2,1,0:T(8,128)(2,1)S(1)}, bf16[384,1024]{1,0:T(8,128)(2,1)S(1)}, bf16[384,1024]{1,0:T(8,128)(2,1)S(1)}) custom-call(bf16[96,1024]{1,0:T(8,128)(2,1)} %x_hbm.1, bf16[96,1024]{1,0:T(8,128)(2,1)} %mlp_hbm.1, bf16[1024,1024]{1,0:T(8,128)(2,1)} %w_hbm.1, f32[4,1024]{1,0:T(4,128)} %bias_hbm.1, bf16[4,1024,1024]{2,1,0:T(8,128)(2,1)} %v_hbm.1), custom_call_target="tpu_custom_call" | custom-call | tf_op jit(solution)/shard_map/exchange/pallas_call | solution.py:485
  92.3 4.6 %finish.1 = (f32[1024,1024]{1,0:T(8,128)}, bf16[4,1024,1024]{2,1,0:T(8,128)(2,1)}) custom-call(bf16[384,1024]{1,0:T(8,128)(2,1)S(1)} %get-tuple-element.5.xg, bf16[384,1024]{1,0:T(8,128)(2,1)S(1)} %get-tuple-element.6.pg, bf16[4,1024,1024]{2,1,0:T(8,128)(2,1)S(1)} %get-tuple-element.7.dec), custom_call_target="tpu_custom_call" | custom-call | tf_op jit(solution)/shard_map/finish/pallas_call | solution.py:541

commit v4 on v3

--- a/solution.py
+++ b/solution.py
@@ -20,9 +20,9 @@
     layers, blocks, chunks, rscale,
     x_hbm, mlp_hbm, w_hbm, bias_hbm, v_hbm,
     dec, xg, pg,
-    mlp, w, bias_all, v, pre, his, hir, los, lor, lat, recon, rss, rsr, og, acc, zds, zdr, ys, yr, bss, bsr,
+    mlp, w, bias_all, v, pre, his, hir, los, lor, lat, recon, rss, rsr, og, acc, zds, zdr, ys, yr, bss, bsr, fas, far,
     x_ss, x_rs, hi_ss, hi_rs, lo_ss, lo_rs, zu_ss, zu_rs, rs_ss, rs_rs, og_ss, og_rs, zd_ss, zd_rs, y_ss, y_rs,
-    fs_ss, fs_rs, bs_ss, bs_rs, own_sem, in_sem,
+    fs_ss, fs_rs, bs_ss, bs_rs, fa_ss, fa_rs, own_sem, in_sem,
 ):
     p = lax.axis_index("layer")
     q = lax.axis_index("latent")
@@ -238,6 +238,16 @@
         zds[l, h, span(j)] = total.astype(BF16)
         zd_copy(l, j, h).start()
 
+    def far_copy(l, h):
+        return rcopy(fas.at[l, h], far.at[t, h], fa_ss.at[l], fa_rs.at[t, h], (p - 2 * (t - l), q))
+
+    def far_in(u, h):
+        return rcopy(fas.at[t, h], far.at[u, h], fa_ss.at[t], fa_rs.at[u, h], (p + 2 * (u - t), q))
+
+    def send_far(l, h, total):
+        fas[l, h] = total.astype(BF16)
+        far_copy(l, h).start()
+
     def send_across(j, h, total):
         acc[t, h, span(j)] = total
         ys[h, span(j)] = total.astype(BF16)
@@ -253,18 +263,19 @@
 
         @pl.when(last)
         def _():
-            bss[span(j)] = back(top - 1, j, other).astype(BF16)
-            bs_copy(j).start()
-
-            @pl.when(j > 0)
-            def _():
-                send_own(j - 1)
-
             def produce(l):
                 for h in range(2):
                     send_down(l, j, h, back(l, j, h))
 
-            loop(0, top - 1, produce)
+            loop(0, min(top - 1, 1), produce)
+            bss[span(j)] = back(top - 1, j, other).astype(BF16)
+            bs_copy(j).start()
+
+            @pl.when(j > 0)
+            def _():
+                send_own(j - 1)
+
+            loop(min(top - 1, 1), top - 1, produce)
             for h in range(2):
                 acc[top, h, span(j)] = back(top, j, h)
             acc[top - 1, y, span(j)] = back(top - 1, j, y)
@@ -277,9 +288,22 @@
         def _():
             def keep(l):
                 for h in range(2):
-                    acc[l, h, span(j)] = back(l, j, h)
+                    total = back(l, j, h)
+                    alone = jnp.logical_and(jnp.logical_and(j == n - 1, l < t), jnp.logical_not(near))
+
+                    @pl.when(alone)
+                    def _():
+                        send_far(l, h, total)
+
+                    @pl.when(jnp.logical_not(alone))
+                    def _():
+                        acc[l, h, span(j)] = total
 
             loop(0, t + 1, keep)
+
+            @pl.when(near)
+            def _():
+                send_across(j, other, acc[t, other, span(j)])
 
     def finish_swap(j):
         bs_copy(j).wait_recv()
@@ -290,28 +314,47 @@
         return acc[l, h, span(j)] + zdr[l, h, span(j)].astype(F32)
 
     def pass_on(j):
+        final = j == n - 1
+
         def add(l):
             for h in range(2):
-                send_down(l, j, h, summed(l, j, h))
-
-            @pl.when(j == n - 1)
+                @pl.when(jnp.logical_not(final))
+                def _():
+                    send_down(l, j, h, summed(l, j, h))
+
+                @pl.when(jnp.logical_and(final, near))
+                def _():
+                    send_far(l, h, summed(l, j, h))
+
+            @pl.when(final)
             def _():
                 dec_piece(l)
 
         loop(0, t, add)
 
     def combine(j):
+        final = j == n - 1
+
         @pl.when(near)
         def _():
-            send_across(j, other, acc[t, other, span(j)])
             send_across(j, y, summed(t, j, y))
 
-        @pl.when(jnp.logical_not(near))
+        @pl.when(jnp.logical_not(jnp.logical_or(near, final)))
         def _():
             for h in range(2):
                 send_across(j, h, summed(t, j, h))
 
-        @pl.when(j == n - 1)
+        @pl.when(jnp.logical_and(final, jnp.logical_not(near)))
+        def _():
+            for h in range(2):
+                def add_far(u):
+                    far_in(u, h).wait_recv()
+                    acc[t, h, span(j)] += far[u, h].astype(F32)
+
+                loop(t + 1, top, add_far)
+                send_across(j, h, acc[t, h, span(j)])
+
+        @pl.when(final)
         def _():
             dec_piece(t)
 
@@ -458,9 +501,18 @@
             def _():
                 settle(lat.at[l, h, pl.ds(0, size * n - apart_rows)], zu_ss.at[l, h])
 
-            @pl.when(jnp.logical_and(l < t, jnp.logical_not(less)))
+            @pl.when(jnp.logical_and(last, jnp.logical_and(l < t, jnp.logical_not(less))))
             def _():
                 settle(zds.at[l, h], zd_ss.at[l, h])
+
+            if n > 1:
+                @pl.when(jnp.logical_and(below, l < t))
+                def _():
+                    settle(zds.at[l, h, pl.ds(0, size * (n - 1))], zd_ss.at[l, h])
+
+        @pl.when(jnp.logical_and(below, l < t))
+        def _():
+            settle(fas.at[l], fa_ss.at[l])
 
     loop(0, t + 1, drain)
 
@@ -482,6 +534,7 @@
     per_side = dma((chunks, 2))
     sides = pltpu.VMEM((2, rows, half), BF16)
     sent = pltpu.VMEM((layers, 2, rows, half), BF16)
+    one_chunk = pltpu.VMEM((layers, 2, rows // chunks, half), BF16)
     return pl.pallas_call(
         functools.partial(exchange_kernel, layers, blocks, chunks, rscale),
         out_shape=(
@@ -505,10 +558,10 @@
             pltpu.VMEM((rows, width), BF16),
             pltpu.VMEM((layers, 2, rows, half), F32),
             sent, sent, sides, sides,
-            pltpu.VMEM((rows, half), BF16), pltpu.VMEM((rows, half), BF16),
+            pltpu.VMEM((rows, half), BF16), pltpu.VMEM((rows, half), BF16), one_chunk, one_chunk,
             one, per_chunk, one, per_side, one, per_chunk, sides_sent, per_layer,
             one, per_chunk, one, per_chunk, sides_sent, per_layer, one, per_side,
-            one, per_chunk, one, per_chunk, one, dma((4,)),
+            one, per_chunk, one, per_chunk, dma((layers,)), dma((layers, 2)), one, dma((4,)),
         ],
         compiler_params=pltpu.CompilerParams(
             collective_id=0, has_side_effects=True, vmem_limit_bytes=40 * 2**20

time: 97.1 us -> 95.4 us (0.982)
  Pallas kernels: 96.3 us -> 94.6 us
    pallas_call x1, Pallas kernels: 91.7 us -> 90 us  [exchange(): pl.pallas_call(functools.partial(exchange_kernel, layers, blocks, chunks,...]
where the time goes in v4:
time: 95.4 us; the launch traced here: 95.2 us
  Pallas kernels  94.6 us (99%)
    pallas_call x1, Pallas kernels, exchange(): pl.pallas_call(functools.partial(exchange_kernel, layers, blocks, chunks,...  90 us
    pallas_call x1, Pallas kernels, local(): pl.pallas_call(finish_kernel, in_specs=[pl.BlockSpec(memory_space=pltpu.V...  4.63 us

profile of v4, /device:TPU:0, one launch (start us, length us, event | category | flops | bytes accessed | tf_op | source)
XLA Modules:
  0.0 95.2 jit_solution(2442477492847037053)
XLA Ops:
  0.6 90.0 %exchange.1 = (bf16[4,1024,1024]{2,1,0:T(8,128)(2,1)S(1)}, bf16[384,1024]{1,0:T(8,128)(2,1)S(1)}, bf16[384,1024]{1,0:T(8,128)(2,1)S(1)}) custom-call(bf16[96,1024]{1,0:T(8,128)(2,1)} %x_hbm.1, bf16[96,1024]{1,0:T(8,128)(2,1)} %mlp_hbm.1, bf16[1024,1024]{1,0:T(8,128)(2,1)} %w_hbm.1, f32[4,1024]{1,0:T(4,128)} %bias_hbm.1, bf16[4,1024,1024]{2,1,0:T(8,128)(2,1)} %v_hbm.1), custom_call_target="tpu_custom_call" | custom-call | tf_op jit(solution)/shard_map/exchange/pallas_call | solution.py:538
  90.6 4.6 %finish.1 = (f32[1024,1024]{1,0:T(8,128)}, bf16[4,1024,1024]{2,1,0:T(8,128)(2,1)}) custom-call(bf16[384,1024]{1,0:T(8,128)(2,1)S(1)} %get-tuple-element.5.xg, bf16[384,1024]{1,0:T(8,128)(2,1)S(1)} %get-tuple-element.6.pg, bf16[4,1024,1024]{2,1,0:T(8,128)(2,1)S(1)} %get-tuple-element.7.dec), custom_call_target="tpu_custom_call" | custom-call | tf_op jit(solution)/shard_map/finish/pallas_call | solution.py:594

commit v5 on v4

--- a/solution.py
+++ b/solution.py
@@ -12,7 +12,7 @@
 BF16 = jnp.bfloat16
 CHUNKS = (6, 3, 2)
 NEAR = 4
-FROM = 1
+FROM = 2
 SWAPS = 2
 
 
@@ -426,12 +426,6 @@
             loop(2, t, lambda d: relay(t - d, i))
 
         j2 = i - back_lag
-        first = jnp.logical_and(last, jnp.logical_and(j2 == 0, n > 1))
-
-        @pl.when(first)
-        def _():
-            backward(j2)
-
         @pl.when(jnp.logical_and(live, t > 1))
         def _():
             relay(0, i)
@@ -448,7 +442,7 @@
         def _():
             own_grad(i)
 
-        @pl.when(jnp.logical_and(jnp.logical_and(j2 >= 0, j2 < n), jnp.logical_not(first)))
+        @pl.when(jnp.logical_and(j2 >= 0, j2 < n))
         def _():
             backward(j2)
 

time: 95.4 us -> 94.5 us (level)
  no operation moved by 1% of the time
where the time goes in v5:
time: 94.5 us; the launch traced here: 94.4 us
  Pallas kernels  93.7 us (99%)
    pallas_call x1, Pallas kernels, exchange(): pl.pallas_call(functools.partial(exchange_kernel, layers, blocks, chunks,...  89.1 us
    pallas_call x1, Pallas kernels, local(): pl.pallas_call(finish_kernel, in_specs=[pl.BlockSpec(memory_space=pltpu.V...  4.63 us

profile of v5, /device:TPU:0, one launch (start us, length us, event | category | flops | bytes accessed | tf_op | source)
XLA Modules:
  0.0 94.4 jit_solution(1869400861145597528)
XLA Ops:
  0.6 89.1 %exchange.1 = (bf16[4,1024,1024]{2,1,0:T(8,128)(2,1)S(1)}, bf16[384,1024]{1,0:T(8,128)(2,1)S(1)}, bf16[384,1024]{1,0:T(8,128)(2,1)S(1)}) custom-call(bf16[96,1024]{1,0:T(8,128)(2,1)} %x_hbm.1, bf16[96,1024]{1,0:T(8,128)(2,1)} %mlp_hbm.1, bf16[1024,1024]{1,0:T(8,128)(2,1)} %w_hbm.1, f32[4,1024]{1,0:T(4,128)} %bias_hbm.1, bf16[4,1024,1024]{2,1,0:T(8,128)(2,1)} %v_hbm.1), custom_call_target="tpu_custom_call" | custom-call | tf_op jit(solution)/shard_map/exchange/pallas_call | solution.py:532
  89.7 4.6 %finish.1 = (f32[1024,1024]{1,0:T(8,128)}, bf16[4,1024,1024]{2,1,0:T(8,128)(2,1)}) custom-call(bf16[384,1024]{1,0:T(8,128)(2,1)S(1)} %get-tuple-element.5.xg, bf16[384,1024]{1,0:T(8,128)(2,1)S(1)} %get-tuple-element.6.pg, bf16[4,1024,1024]{2,1,0:T(8,128)(2,1)S(1)} %get-tuple-element.7.dec), custom_call_target="tpu_custom_call" | custom-call | tf_op jit(solution)/shard_map/finish/pallas_call | solution.py:588

commit v6 on v5

--- a/solution.py
+++ b/solution.py
@@ -376,7 +376,7 @@
 
     grad_lag = jnp.where(last, 1, 2)
     back_lag = jnp.where(last, 1, 3)
-    sum_lag = jnp.where(last, 1, jnp.where(near, NEAR, max(n, NEAR)))
+    sum_lag = jnp.where(last, 1, jnp.where(near, NEAR, max(n - 1, NEAR)))
     own_latents(0)
     loop(early, ahead, encode)
     v_copy.wait()

time: 94.5 us -> 94.5 us (level)
  no operation moved by 1% of the time
where the time goes in v6:
time: 94.5 us; the launch traced here: 94.4 us
  Pallas kernels  93.7 us (99%)
    pallas_call x1, Pallas kernels, exchange(): pl.pallas_call(functools.partial(exchange_kernel, layers, blocks, chunks,...  89.1 us
    pallas_call x1, Pallas kernels, local(): pl.pallas_call(finish_kernel, in_specs=[pl.BlockSpec(memory_space=pltpu.V...  4.63 us

profile of v6, /device:TPU:0, one launch (start us, length us, event | category | flops | bytes accessed | tf_op | source)
XLA Modules:
  0.0 94.4 jit_solution(1625281319501308575)
XLA Ops:
  0.6 89.1 %exchange.1 = (bf16[4,1024,1024]{2,1,0:T(8,128)(2,1)S(1)}, bf16[384,1024]{1,0:T(8,128)(2,1)S(1)}, bf16[384,1024]{1,0:T(8,128)(2,1)S(1)}) custom-call(bf16[96,1024]{1,0:T(8,128)(2,1)} %x_hbm.1, bf16[96,1024]{1,0:T(8,128)(2,1)} %mlp_hbm.1, bf16[1024,1024]{1,0:T(8,128)(2,1)} %w_hbm.1, f32[4,1024]{1,0:T(4,128)} %bias_hbm.1, bf16[4,1024,1024]{2,1,0:T(8,128)(2,1)} %v_hbm.1), custom_call_target="tpu_custom_call" | custom-call | tf_op jit(solution)/shard_map/exchange/pallas_call | solution.py:532
  89.7 4.6 %finish.1 = (f32[1024,1024]{1,0:T(8,128)}, bf16[4,1024,1024]{2,1,0:T(8,128)(2,1)}) custom-call(bf16[384,1024]{1,0:T(8,128)(2,1)S(1)} %get-tuple-element.5.xg, bf16[384,1024]{1,0:T(8,128)(2,1)S(1)} %get-tuple-element.6.pg, bf16[4,1024,1024]{2,1,0:T(8,128)(2,1)S(1)} %get-tuple-element.7.dec), custom_call_target="tpu_custom_call" | custom-call | tf_op jit(solution)/shard_map/finish/pallas_call | solution.py:588
